TPU v7x, 512 devices: a whole 4x8x8 slice. The times are simulated.
512 devices in a mesh: stretch: 4 (over y_lo), seq: 128 (over z, y_hi, x, core).
Axes of the slice: x: 4, y: 8 (y_hi: 2, y_lo: 4; y = y_hi * 4 + y_lo), z: 8, core: 2. Of those that a mesh axis runs over, the one named last changes fastest.
Arguments:
- query_rows: bfloat16 [4, 4096, 4096], P('stretch', 'seq'), may hold values from -160 to 160
- key_rows: bfloat16 [4, 4096, 4096], P('stretch', 'seq'), may hold values from -5 to 5
- value_rows: bfloat16 [4, 4096, 4096], P('stretch', 'seq'), may hold values from -6 to 6
- cache_from: int32 [4], P('stretch'), may hold values from 0 to 4095
- time_index: int32 [4], P('stretch'), may hold values from 0 to 49
- gate_table: float32 [50, 4096], replicated, may hold values from 4 to 16
Outputs:
- attn_out: bfloat16 [4, 4096, 4096], P('stretch', 'seq')
All inputs are finite; a program needn't handle non-finite values.
Results may differ from a plain program's by a relative error of at most 0.0055.
Values may be sent and summed in bfloat16 or wider, within the bound.
A program may use at most 64 MiB of HBM per device.

v0:
```python
import math

import jax
import jax.numpy as jnp
from jax import lax
from jax.sharding import Mesh
from jax.sharding import PartitionSpec as P

HEADS = 32
HD = 128
SEQ = ("seq_0", "seq_1", "seq_2", "seq_3")


def in_one_piece(arrays, axis, split_dim, concat_dim, along):
    widths = [a.shape[along] for a in arrays]
    both = jnp.concatenate(arrays, axis=along)
    filled = lax.all_to_all(both, axis, split_axis=split_dim, concat_axis=concat_dim, tiled=True)
    return tuple(jnp.split(filled, [sum(widths[:k]) for k in range(1, len(widths))], axis=along))


def passed_along(block, axis, distance):
    devices = range(lax.axis_size(axis))
    route = [(i - distance, i) for i in devices if i - distance in devices]
    return lax.ppermute(block, axis, route)


def in_blocks(x, dim, size):
    lengths = x.shape
    parts = x.reshape(*lengths[:dim], size, lengths[dim] // size, *lengths[dim + 1 :])
    return jnp.moveaxis(parts, dim, 0)


def joined_along(parts, dim):
    parts = jnp.moveaxis(parts, 0, dim)
    lengths = parts.shape
    return parts.reshape(*lengths[:dim], lengths[dim] * lengths[dim + 1], *lengths[dim + 2 :])


def moved_by_axis(parts, axes, order):
    lengths = [lax.axis_size(a) for a in axes]
    parts = parts.reshape(*lengths, *parts.shape[1:])
    for k in order:
        parts = lax.all_to_all(parts, axes[k], split_axis=k, concat_axis=k, tiled=True)
    return parts.reshape(-1, *parts.shape[len(axes) :])


def two_step_exchange(x, groups, order, split_dim, concat_dim):
    size = lax.axis_size(groups[0]) * lax.axis_size(groups[1])
    parts = in_blocks(x, split_dim, size)
    return joined_along(moved_by_axis(parts, groups, order), concat_dim)


def spread(rows, groups, per_dev, blocks):
    count = rows.shape[0]
    arranged = rows.reshape(count, groups, per_dev, HD).transpose(1, 0, 2, 3)
    return jnp.repeat(arranged, blocks, axis=0)


def body(query_rows, key_rows, value_rows, cache_from, time_index, gate_table):
    seq_count = lax.axis_size(SEQ)
    own_count = query_rows.shape[1]
    blocks = max(seq_count // HEADS, 1)
    per_dev = HEADS * blocks // seq_count
    groups = HEADS // per_dev
    part_len = own_count // blocks
    queries = query_rows[0].reshape(blocks, part_len, groups, per_dev, HD).transpose(2, 0, 1, 3, 4)
    queries = queries.reshape(groups * blocks, part_len, per_dev, HD)
    got_query, got_key, got_value = (
        lax.all_to_all(queries, SEQ, split_axis=0, concat_axis=1, tiled=True),
        *in_one_piece(
            (
                spread(key_rows[0], groups, per_dev, blocks),
                spread(value_rows[0], groups, per_dev, blocks),
            ),
            SEQ,
            0,
            1,
            2,
        ),
    )
    got_past_key, got_past_value = passed_along((got_key, got_value), "stretch", 1)
    head_queries = got_query[0]
    total_tokens = got_key.shape[1]
    position = jnp.arange(total_tokens)
    later = lax.axis_index("stretch") > 0
    past_visible = jnp.logical_and(position >= cache_from[0], later)
    visible = jnp.concatenate([jnp.ones((total_tokens,), bool), past_visible])
    keys_all = jnp.concatenate([got_key[0], got_past_key[0]], 0)
    values_all = jnp.concatenate([got_value[0], got_past_value[0]], 0)
    span = math.gcd(512, 2 * total_tokens)
    count_blocks = 2 * total_tokens // span
    key_blocks = keys_all.reshape(count_blocks, span, per_dev, HD)
    value_blocks = values_all.reshape(count_blocks, span, per_dev, HD)
    visible_blocks = visible.reshape(count_blocks, span)
    query_count = head_queries.shape[0]
    scale = HD ** (-0.5)

    def absorb(carry, packed):
        largest, total, numer = carry
        key_block, value_block, seen = packed
        scores = (
            jnp.einsum("qhd,khd->hqk", head_queries, key_block, preferred_element_type=jnp.float32)
            * scale
        )
        scores = jnp.where(seen[None, None, :], scores, -1e30)
        updated = jnp.maximum(largest, jnp.max(scores, axis=2))
        factor = jnp.exp(largest - updated)
        weights = jnp.where(seen[None, None, :], jnp.exp(scores - updated[:, :, None]), 0.0)
        total = total * factor + jnp.sum(weights, axis=2)
        numer = numer * jnp.transpose(factor)[:, :, None] + jnp.einsum(
            "hqk,khd->qhd",
            weights.astype(jnp.bfloat16),
            value_block,
            preferred_element_type=jnp.float32,
        )
        return ((updated, total, numer), None)

    initial = (
        jnp.full((per_dev, query_count), -1e30, jnp.float32),
        jnp.zeros((per_dev, query_count), jnp.float32),
        jnp.zeros((query_count, per_dev, HD), jnp.float32),
    )
    (largest, total, numer), unused = lax.scan(
        absorb, initial, (key_blocks, value_blocks, visible_blocks)
    )
    attended = (numer / jnp.transpose(total)[:, :, None]).astype(jnp.bfloat16)
    returned = two_step_exchange(
        attended[None], (("seq_0", "seq_1", "seq_2"), "seq_3"), (1, 0), 1, 0
    )
    tokens_out = returned.reshape(groups, blocks, part_len, per_dev, HD).transpose(1, 2, 0, 3, 4)
    tokens_out = tokens_out.reshape(own_count, HEADS * HD)
    matched = jnp.arange(gate_table.shape[0]) == time_index[0]
    gate_row = jnp.sum(jnp.where(matched[:, None], gate_table, 0.0), axis=0)
    attn_out = (tokens_out.astype(jnp.float32) * gate_row).astype(jnp.bfloat16)[None]
    return attn_out


def solution(mesh):
    finer = Mesh(
        mesh.devices.reshape(mesh.shape["stretch"], 8, 2, 4, 2),
        ("stretch", "seq_0", "seq_1", "seq_2", "seq_3"),
    )
    placed = (
        P("stretch", SEQ, None),
        P("stretch", SEQ, None),
        P("stretch", SEQ, None),
        P("stretch"),
        P("stretch"),
        P(),
    )
    return jax.shard_map(
        body, mesh=finer, in_specs=placed, out_specs=P("stretch", SEQ, None), check_vma=False
    )
```

profile of v0, /device:TPU:1, one launch (start us, length us, event | category | flops | bytes accessed | tf_op | source)
XLA Modules:
  0.0 226.3 jit_solution(11351040144100769614)
XLA Ops:
  2.8 72.5 %all_to_all.31 = bf16[128,32,2,128]{3,1,2,0:T(8,128)(2,1)S(1)} all-to-all(bf16[128,32,2,128]{3,1,2,0:T(8,128)(2,1)S(1)} %pad_maximum_fusion), channel_id=1, replica_groups=mesh['stretch'=4,'seq_0'=8,'seq_1'=2,'seq_2'=4,'seq_3'=2] {'seq_0','seq_..., dimensions={0} | all-to-all | bytes 4194304 | tf_op jit(solution)/shard_map/all_to_all | solution.py:17
  75.6 1.5 slice_bitcast_fusion
  77.2 9.4 %collective-permute-start.1 = (bf16[1,4096,1,128]{3,1,2,0:T(8,128)(2,1)}, bf16[1,4096,1,128]{3,1,2,0:T(8,128)(2,1)}, u32[]{:S(2)}, u32[]{:S(2)}) collective-permute-start(bf16[1,4096,1,128]{3,1,2,0:T(8,128)(2,1)} %get-tuple-element.131), channel_id=1, source_target_pairs={{0,128},{128,256},{256,384},{1,129},{129,257},{257,385},{2,130},{1... | collective-permute-start | bytes 3145736 | tf_op jit(solution)/shard_map/ppermute | solution.py:24
  87.3 7.4 %all-to-all-start.1 = ((bf16[128,8,1,128]{3,1,2,0:T(8,128)(2,1)}), bf16[128,8,1,128]{3,1,2,0:T(8,128)(2,1)S(1)}, u32[]{:S(2)}, u32[]{:S(2)}) async-start(bf16[128,8,1,128]{3,1,2,0:T(8,128)(2,1)} %bitcast.14), calls=%async_computation.1 | async-start | bytes 524288 | tf_op jit(solution)/shard_map/all_to_all | solution.py:69
  95.5 2.3 %collective-permute-start = (bf16[1,4096,1,128]{3,1,2,0:T(8,128)(2,1)S(1)}, bf16[1,4096,1,128]{3,1,2,0:T(8,128)(2,1)}, u32[]{:S(2)}, u32[]{:S(2)}) collective-permute-start(bf16[1,4096,1,128]{3,1,2,0:T(8,128)(2,1)S(1)} %get-tuple-element.132), channel_id=1, source_target_pairs={{0,128},{128,256},{256,384},{1,129},{129,257},{257,385},{2,130},{1... | collective-permute-start | bytes 3145736 | tf_op jit(solution)/shard_map/ppermute | solution.py:24
  97.8 13.3 %collective-permute-done.1 = bf16[1,4096,1,128]{3,1,2,0:T(8,128)(2,1)} collective-permute-done((bf16[1,4096,1,128]{3,1,2,0:T(8,128)(2,1)}, bf16[1,4096,1,128]{3,1,2,0:T(8,128)(2,1)}, u32[]{:S(2)}, u32[]{:S(2)}) %collective-permute-start.1) | collective-permute-done | bytes 1048608 | tf_op jit(solution)/shard_map/ppermute | solution.py:24
  111.1 2.7 %pad_maximum_fusion.2 = bf16[8192,1,128]{2,0,1:T(8,128)(2,1)} fusion(bf16[4096,1,128]{2,0,1:T(8,128)(2,1)} %bitcast.17, bf16[4096,1,128]{2,0,1:T(8,128)(2,1)S(1)} %get-tuple-element.129), kind=kLoop, calls=%fused_computation.32 | loop fusion | flops 4194304 | bytes 4194304 | tf_op jit(solution)/shard_map/concatenate | solution.py:89
  113.8 22.5 %collective-permute-done = bf16[1,4096,1,128]{3,1,2,0:T(8,128)(2,1)} collective-permute-done((bf16[1,4096,1,128]{3,1,2,0:T(8,128)(2,1)S(1)}, bf16[1,4096,1,128]{3,1,2,0:T(8,128)(2,1)}, u32[]{:S(2)}, u32[]{:S(2)}) %collective-permute-start) | collective-permute-done | bytes 1048608 | tf_op jit(solution)/shard_map/ppermute | solution.py:24
  136.3 2.7 %pad_maximum_fusion.1 = bf16[8192,1,128]{2,0,1:T(8,128)(2,1)} fusion(bf16[4096,1,128]{2,0,1:T(8,128)(2,1)} %bitcast.9, bf16[4096,1,128]{2,0,1:T(8,128)(2,1)S(1)} %get-tuple-element.130), kind=kLoop, calls=%fused_computation.31 | loop fusion | flops 4194304 | bytes 4194304 | tf_op jit(solution)/shard_map/concatenate | solution.py:88
  139.0 60.6 %while.15 = (s32[]{:T(128)}, f32[1,1024]{1,0:T(1,128)S(1)}, f32[1,1024]{1,0:T(1,128)S(1)}, f32[1024,1,128]{0,2,1:T(8,128)S(1)}, pred[16,512]{1,0:T(8,128)(4,1)S(...) while((s32[]{:T(128)}, f32[1,1024]{1,0:T(1,128)S(1)}, ...), condition=%wide.region_3.4_spmd.clone, body=%wide.region_0.3_spmd.clone.sunk | while | flops 275649536 | bytes 7933557 | solution.py:123
  139.0 1.4 fusion.34
  141.0 1.7 fusion.38
  144.8 1.7 fusion.38
  148.6 1.7 fusion.38
  150.4 1.4 fusion.34
  152.4 1.7 fusion.38
  156.2 1.7 fusion.38
  160.0 1.7 fusion.38
  163.7 1.7 fusion.38
  167.5 1.7 fusion.38
  171.3 1.7 fusion.38
  173.1 1.4 fusion.34
  175.1 1.7 fusion.38
  178.9 1.7 fusion.38
  182.7 1.7 fusion.38
  186.5 1.7 fusion.38
  190.3 1.7 fusion.38
  194.1 1.7 fusion.38
  197.9 1.7 fusion.38
  200.1 4.5 %all_to_all.32 = bf16[64,2,1,8,1,128]{5,3,0,4,2,1:T(8,128)(2,1)S(1)} all-to-all(bf16[64,2,1,8,1,128]{5,3,0,4,2,1:T(8,128)(2,1)S(1)} %copy.43), channel_id=1, replica_groups=mesh['stretch'=4,'seq_0'=8,'seq_1'=2,'seq_2'=4,'seq_3'=2] {'seq_3'}, dimensions={1} | all-to-all | bytes 524288 | tf_op jit(solution)/shard_map/all_to_all | solution.py:43
  205.4 5.4 %all-to-all-start.3 = ((bf16[64,2,1,8,1,128]{5,3,1,4,2,0:T(8,128)(2,1)}), bf16[64,2,1,8,1,128]{5,3,1,4,2,0:T(8,128)(2,1)S(1)}, u32[]{:S(2)}, u32[]{:S(2)}) async-start(bf16[64,2,1,8,1,128]{5,3,1,4,2,0:T(8,128)(2,1)} %copy.44), calls=%async_computation.3 | async-start | bytes 524288 | tf_op jit(solution)/shard_map/all_to_all | solution.py:43
  211.6 13.3 %all-to-all-done.3 = bf16[64,2,1,8,1,128]{5,3,1,4,2,0:T(8,128)(2,1)S(1)} async-done(((bf16[64,2,1,8,1,128]{5,3,1,4,2,0:T(8,128)(2,1)}), bf16[64,2,1,8,1,128]{5,3,1,4,2,0:T(8,128)(2,1)S(1)}, u32[]{:S(2)}, u32[]{:S(2)}) %all-to-all-start.3) | async-done | bytes 262176 | tf_op jit(solution)/shard_map/all_to_all | solution.py:43
  (124 shorter events, 34.3 us)
Async XLA Ops:
  75.6 10.9 %copy-start.2 = (bf16[1,32,4096]{2,1,0:T(8,128)(2,1)S(1)}, bf16[1,32,4096]{2,1,0:T(8,128)(2,1)}, u32[]{:S(2)}) copy-start(bf16[1,32,4096]{2,1,0:T(8,128)(2,1)} %param.8) | copy-start | bytes 786436
  77.2 33.9 %collective-permute-start.1 = (bf16[1,4096,1,128]{3,1,2,0:T(8,128)(2,1)}, bf16[1,4096,1,128]{3,1,2,0:T(8,128)(2,1)}, u32[]{:S(2)}, u32[]{:S(2)}) collective-permute-start(bf16[1,4096,1,128]{3,1,2,0:T(8,128)(2,1)} %get-tuple-element.131), channel_id=1, source_target_pairs={{0,128},{128,256},{256,384},{1,129},{129,257},{257,385},{2,130},{1... | collective-permute-start | bytes 3145736 | tf_op jit(solution)/shard_map/ppermute | solution.py:24
  87.3 51.7 %all-to-all-start.1 = ((bf16[128,8,1,128]{3,1,2,0:T(8,128)(2,1)}), bf16[128,8,1,128]{3,1,2,0:T(8,128)(2,1)S(1)}, u32[]{:S(2)}, u32[]{:S(2)}) async-start(bf16[128,8,1,128]{3,1,2,0:T(8,128)(2,1)} %bitcast.14), calls=%async_computation.1 | async-start | bytes 524288 | tf_op jit(solution)/shard_map/all_to_all | solution.py:69
  95.5 40.8 %collective-permute-start = (bf16[1,4096,1,128]{3,1,2,0:T(8,128)(2,1)S(1)}, bf16[1,4096,1,128]{3,1,2,0:T(8,128)(2,1)}, u32[]{:S(2)}, u32[]{:S(2)}) collective-permute-start(bf16[1,4096,1,128]{3,1,2,0:T(8,128)(2,1)S(1)} %get-tuple-element.132), channel_id=1, source_target_pairs={{0,128},{128,256},{256,384},{1,129},{129,257},{257,385},{2,130},{1... | collective-permute-start | bytes 3145736 | tf_op jit(solution)/shard_map/ppermute | solution.py:24
  136.3 2.7 %copy-start.1 = (f32[1024,1,128]{0,2,1:T(8,128)S(1)}, f32[1024,1,128]{0,2,1:T(8,128)}, u32[]{:S(2)}) copy-start(f32[1024,1,128]{0,2,1:T(8,128)} %custom-call.2) | copy-start | bytes 1572868
  199.6 11.8 %copy-start = (f32[50,4096]{1,0:T(8,128)S(1)}, f32[50,4096]{1,0:T(8,128)}, u32[]{:S(2)}) copy-start(f32[50,4096]{1,0:T(8,128)} %param.13) | copy-start | bytes 2457604
  205.4 19.5 %all-to-all-start.3 = ((bf16[64,2,1,8,1,128]{5,3,1,4,2,0:T(8,128)(2,1)}), bf16[64,2,1,8,1,128]{5,3,1,4,2,0:T(8,128)(2,1)S(1)}, u32[]{:S(2)}, u32[]{:S(2)}) async-start(bf16[64,2,1,8,1,128]{5,3,1,4,2,0:T(8,128)(2,1)} %copy.44), calls=%async_computation.3 | async-start | bytes 524288 | tf_op jit(solution)/shard_map/all_to_all | solution.py:43
where the time goes:
time: 230 us; the launch traced here: 226 us
  blocking collectives  77.1 us (34%)
  matrix products  49.6 us (22%)
  waiting for transfers between devices  49.1 us (21%)
  starting transfers between devices  24.5 us (11%)
  other arithmetic  16.7 us (7%)
  local copies, waits for them, and re-layouts  6.95 us (3%)
    all_to_all x1, blocking collectives, in_one_piece(): lax.all_to_all(both, axis, split_axis=split_dim, concat_axis=concat_dim,...  72.5 us
    ppermute x2, waiting for transfers between devices, passed_along(): return lax.ppermute(block, axis, route)  35.8 us
    dot_general x16, matrix products, absorb(): jnp.einsum('hqk,khd->qhd', weights.astype(jnp.bfloat16), value_block, pre...  27.9 us
    dot_general x16, matrix products, absorb(): jnp.einsum('qhd,khd->hqk', head_queries, key_block, preferred_element_typ...  21.7 us
    all_to_all x1, waiting for transfers between devices, moved_by_axis(): lax.all_to_all(parts, axes[k], split_axis=k, concat_axis=k, tiled=True)  13.3 us
    ppermute x2, starting transfers between devices, passed_along(): return lax.ppermute(block, axis, route)  11.7 us
    reduce_sum x16, other arithmetic, absorb(): total = total * factor + jnp.sum(weights, axis=2)  9.04 us
    all_to_all x1, starting transfers between devices, body(): lax.all_to_all(queries, SEQ, split_axis=0, concat_axis=1, tiled=True)  7.45 us
  transfers between devices with their start and end apart: 4, of which 3 were waited for; matrix products, arithmetic and copies ran while one was open for 3% of the time, Pallas kernels for 0%

commit v1 on v0

v1 whole, which is shorter than its diff:
```python
import functools
import math

import jax
import jax.numpy as jnp
from jax import lax
from jax.experimental import pallas as pl
from jax.experimental.pallas import tpu as pltpu
from jax.sharding import Mesh
from jax.sharding import PartitionSpec as P

HEADS = 32
HD = 128
AXES = ("stretch", "z", "yh", "xh", "xl", "co")
SEQ = AXES[1:]
MESH = pl.DeviceIdType.MESH
NEG = -1e30
LOG2 = HD**-0.5 * math.log2(math.e)
NT = (((1,), (1,)), ((), ()))


def to_row(column):
    return jnp.broadcast_to(column, (128, 128)).T[0:1, :]


def to_column(row):
    return jnp.broadcast_to(row, (128, 128)).T[:, 0:1]


def kernel(
    q_in, k_in, v_in, cf_ref, att,
    q1, k1, v1, qb, qp, kb, vb, cfb, cf_in, bias, op, op_in, st, st_in, ob, r1,
    s1, r1s, l1, s2, r2s, l2, gs, gr, hs, hr, os_, or_, zs, zr, lo, fs, fr, lf,
):
    c, z, yh, xh, xl, co = (lax.axis_index(a) for a in AXES)
    g = yh * 2 + xh
    half = z // 4

    def dev(c=c, z=z, g=g, xl=xl, co=co):
        return (c, z, g // 2, lax.rem(g, 2), xl, co)

    def gx(d):
        return ((yh + d // 2) % 2) * 2 + (xh + d % 2) % 2

    before = lax.rem(c + 3, 4)
    after = lax.rem(c + 1, 4)
    twin = dev(co=1 - co)
    across = dev(xl=1 - xl)

    for slot in range(4):
        vb[slot, :, :, :, HD:] = jnp.ones((8, 4, 32, HD), jnp.bfloat16)
    cfb[...] = jnp.full((8, 128), cf_ref[0], jnp.float32)

    barrier = pltpu.get_barrier_semaphore()
    partners = [dev(z=lax.rem(z + d, 8)) for d in range(1, 8)]
    partners += [dev(g=gx(d)) for d in range(1, 4)]
    partners += [twin, across, dev(c=before), dev(c=after)]
    for partner in partners:
        pl.semaphore_signal(barrier, inc=1, device_id=partner, device_id_type=MESH)
    pl.semaphore_wait(barrier, len(partners))

    def remote(src, dst, send, recv, to):
        return pltpu.make_async_remote_copy(
            src_ref=src, dst_ref=dst, send_sem=send, recv_sem=recv, device_id=to, device_id_type=MESH
        )

    def lanes(start, size):
        return pl.ds(pl.multiple_of(start, 128), size)

    sent = []
    first = []
    for n, (src, dst) in enumerate(((q_in, q1), (k_in, k1), (v_in, v1))):
        copies = [
            remote(src.at[:, lanes(gx(d) * 1024, 1024)], dst.at[g], s1.at[n, d - 1], r1s.at[n, d - 1], dev(g=gx(d)))
            for d in (3, 2, 1)
        ]
        own = pltpu.make_async_copy(src.at[:, lanes(g * 1024, 1024)], dst.at[g], l1.at[n])
        for copy in copies:
            copy.start()
        own.start()
        first.append((copies, own))
        sent += copies

    def second(n, src, dst):
        copies = [
            remote(
                src.at[:, :, lanes(lax.rem(z + d, 8) * HD, HD)], dst(z), s2.at[n, d - 1], r2s.at[n, d - 1],
                dev(z=lax.rem(z + d, 8)),
            )
            for d in (4, 3, 5, 2, 6, 1, 7)
        ]
        own = pltpu.make_async_copy(src.at[:, :, lanes(z * HD, HD)], dst(z), l2.at[n])
        for copy in copies:
            copy.start()
        own.start()
        sent.extend(copies)
        return copies, own

    def arrived(stage):
        copies, own = stage
        for copy in copies:
            copy.wait_recv()
        own.wait()

    def gather(n, buf, cols):
        to_twin = remote(buf.at[0, :, :, :, cols], buf.at[1, :, :, :, cols], gs.at[n, 0], gr.at[n, 0], twin)
        to_across = remote(buf.at[0, :, :, :, cols], buf.at[2, :, :, :, cols], gs.at[n, 1], gr.at[n, 1], across)
        relay = remote(buf.at[2, :, :, :, cols], buf.at[3, :, :, :, cols], gs.at[n, 2], gr.at[n, 2], twin)
        to_across.start()
        to_twin.start()
        sent.extend((to_twin, to_across, relay))
        return to_twin, to_across, relay

    cols = pl.ds(0, HD)
    for slot in range(4):
        vb[slot, :, :, :, HD:] = jnp.ones((8, 4, 32, HD), jnp.bfloat16)
    @pl.when(c == 0)
    def _():
        op_in[...] = jnp.zeros_like(op_in)
        st_in[:, 0:4, :] = jnp.full((2, 4, 128), NEG, jnp.float32)
        st_in[:, 4:8, :] = jnp.zeros((2, 4, 128), jnp.float32)

    arrived(first[0])
    q_stage = second(0, q1, lambda i: qb.at[i])
    arrived(first[1])
    k_stage = second(1, k1, lambda i: kb.at[0, i])
    arrived(q_stage)
    q_hop = remote(qb, qp, hs.at[0], hr.at[0], dev(c=before))
    cf_hop = remote(cfb, cf_in, hs.at[1], hr.at[1], dev(c=before))

    @pl.when(c > 0)
    def _():
        q_hop.start()
        cf_hop.start()

    arrived(first[2])
    v_stage = second(2, v1, lambda i: vb.at[0, i, :, :, cols])
    arrived(k_stage)
    k_twin, k_across, k_relay = gather(0, kb, cols)
    arrived(v_stage)
    v_twin, v_across, v_relay = gather(1, vb, cols)
    k_across.wait_recv()
    k_relay.start()
    k_twin.wait_recv()
    v_across.wait_recv()
    v_relay.start()
    v_twin.wait_recv()
    k_relay.wait_recv()
    v_relay.wait_recv()

    def attend(queries, masked):
        largest = None
        for slot in range(4):
            for part in range(2):
                keys = kb[slot, part * 4 : part * 4 + 4].reshape(512, HD)
                values = vb[slot, part * 4 : part * 4 + 4].reshape(512, 2 * HD)
                scores = lax.dot_general(queries, keys, NT, preferred_element_type=jnp.float32)
                if masked:
                    scores = scores + bias[slot : slot + 1, part * 512 : part * 512 + 512]
                here = jnp.max(scores, axis=1, keepdims=True)
                updated = here if largest is None else jnp.maximum(largest, here)
                weights = jnp.exp2((scores - updated) * LOG2).astype(jnp.bfloat16)
                more = jnp.dot(weights, values, preferred_element_type=jnp.float32)
                numer = more if largest is None else numer * jnp.exp2((largest - updated) * LOG2) + more
                largest = updated
        return largest, numer[:, HD : HD + 1], numer[:, :HD]

    returns = [
        (
            remote(op.at[pl.ds(i * 4, 4)], op_in.at[pl.ds(i * 4, 4)], os_.at[i], or_.at[i], dev(c=after)),
            remote(st.at[i], st_in.at[i], os_.at[2 + i], or_.at[2 + i], dev(c=after)),
        )
        for i in range(2)
    ]

    @pl.when(c < 3)
    def _():
        q_hop.wait_recv()
        cf_hop.wait_recv()
        cache_from = cf_in[0:1, 0:1]
        for slot in range(4):
            chunk = lax.rem(xl + slot // 2, 2) * 2 + lax.rem(co + slot % 2, 2)
            row = lax.broadcasted_iota(jnp.int32, (1, 1024), 1)
            position = (row // 32) * 128 + chunk * 32 + row % 32
            bias[pl.ds(slot, 1), :] = jnp.where(position.astype(jnp.float32) >= cache_from, 0.0, NEG)
        for i in range(2):
            largest, total, numer = attend(qp[i * 4 : i * 4 + 4].reshape(512, HD), True)
            op[pl.ds(i * 4, 4)] = (numer / total).astype(jnp.bfloat16).reshape(4, 4, 32, HD)
            for n in range(4):
                rows = slice(n * 128, n * 128 + 128)
                st[i, n : n + 1, :] = to_row(largest[rows])
                st[i, n + 4 : n + 5, :] = to_row(total[rows])
            for copy in returns[i]:
                copy.start()

    pieces = []

    def pass_on(sender):
        head = (g * 8 + sender) * HD
        for d in (3, 2, 1):
            copy = remote(r1.at[sender, gx(d)], att.at[:, lanes(head, HD)], fs.at[d - 1], fr.at[d - 1], dev(g=gx(d)))
            copy.start()
        pltpu.make_async_copy(r1.at[sender, g], att.at[:, lanes(head, HD)], lf.at[0]).start()

    for i in range(2):
        base = (half + 1 - i) % 2
        rows4 = pl.ds(base * 4, 4)
        largest, total, numer = attend(qb[rows4].reshape(512, HD), False)

        if i == 0:

            @pl.when(c > 0)
            def _():
                for j in range(2):
                    for copy in returns[j]:
                        copy.wait_recv()

        past = op_in[rows4].reshape(512, HD).astype(jnp.float32)
        stats = st_in[base]
        past_largest = jnp.concatenate([to_column(stats[n : n + 1]) for n in range(4)], 0)
        past_total = jnp.concatenate([to_column(stats[n + 4 : n + 5]) for n in range(4)], 0)
        updated = jnp.maximum(largest, past_largest)
        mine = jnp.exp2((largest - updated) * LOG2)
        theirs = past_total * jnp.exp2((past_largest - updated) * LOG2)
        whole = (numer * mine + past * theirs) / (total * mine + theirs)
        ob[rows4] = whole.astype(jnp.bfloat16).reshape(4, 4, 32, HD)
        steps = (0, 1, 2, 3) if i == 0 else (1, 2, 3)
        for k in steps:
            to = base * 4 + (z + k) % 4
            copy = remote(ob.at[to], r1.at[z], zs.at[i * 4 + k], zr.at[z], dev(z=to))
            copy.start()
            pieces.append(copy)
        if i == 1:
            own = pltpu.make_async_copy(ob.at[z], r1.at[z], lo.at[0])
            own.start()
        for k in steps:
            sender = base * 4 + (z + k) % 4
            remote(ob.at[0], r1.at[sender], zs.at[0], zr.at[sender], dev(z=sender)).wait_recv()
            pass_on(sender)
        if i == 1:
            own.wait()
            pass_on(z)

    all_rows = att.at[:, pl.ds(0, 1024)]
    pltpu.make_async_copy(all_rows, all_rows, lf.at[0]).wait()
    for d in (1, 2, 3):
        remote(all_rows, all_rows, fs.at[d - 1], fr.at[d - 1], twin).wait()
    for copy in sent + pieces:
        copy.wait_send()

    @pl.when(c > 0)
    def _():
        q_hop.wait_send()
        cf_hop.wait_send()

    @pl.when(c < 3)
    def _():
        for i in range(2):
            for copy in returns[i]:
                copy.wait_send()


def body(query_rows, key_rows, value_rows, cache_from, time_index, gate_table):
    bf16, f32, dma = jnp.bfloat16, jnp.float32, pltpu.SemaphoreType.DMA
    vmem = pl.BlockSpec(memory_space=pltpu.VMEM)
    hbm = pl.BlockSpec(memory_space=pltpu.HBM)
    attended = pl.pallas_call(
        kernel,
        out_shape=jax.ShapeDtypeStruct((32, HEADS * HD), bf16),
        in_specs=[hbm, hbm, hbm, pl.BlockSpec(memory_space=pltpu.SMEM)],
        out_specs=vmem,
        scratch_shapes=[
            *[pltpu.VMEM((4, 32, 1024), bf16)] * 3,
            *[pltpu.VMEM((8, 4, 32, HD), bf16)] * 2,
            pltpu.VMEM((4, 8, 4, 32, HD), bf16),
            pltpu.VMEM((4, 8, 4, 32, 2 * HD), bf16),
            *[pltpu.VMEM((8, 128), f32)] * 2,
            pltpu.VMEM((8, 1024), f32),
            *[pltpu.VMEM((8, 4, 32, HD), bf16)] * 2,
            *[pltpu.VMEM((2, 8, 128), f32)] * 2,
            *[pltpu.VMEM((8, 4, 32, HD), bf16)] * 2,
            dma((3, 3)), dma((3, 3)), dma((3,)),
            dma((3, 7)), dma((3, 7)), dma((3,)),
            dma((2, 3)), dma((2, 3)),
            dma((2,)), dma((2,)),
            dma((4,)), dma((4,)),
            dma((8,)), dma((8,)), dma((1,)),
            dma((3,)), dma((3,)), dma((1,)),
        ],
        compiler_params=pltpu.CompilerParams(
            collective_id=1, has_side_effects=True
        ),
    )(query_rows[0], key_rows[0], value_rows[0], cache_from)
    gate_row = lax.dynamic_slice_in_dim(gate_table, time_index[0], 1, 0)
    return (attended.astype(jnp.float32) * gate_row).astype(jnp.bfloat16)[None]


def solution(mesh):
    finer = Mesh(mesh.devices.reshape(4, 8, 2, 2, 2, 2), AXES)
    rows = P("stretch", SEQ, None)
    return jax.shard_map(
        body,
        mesh=finer,
        in_specs=(rows, rows, rows, P("stretch"), P("stretch"), P()),
        out_specs=rows,
        check_vma=False,
    )
```

time: 230 us -> 91.3 us (0.40)
  the two profiles are of different devices: /device:TPU:1 before, /device:TPU:56 now
where the time goes in v1:
time: 91.3 us; the launch traced here: 91.1 us
  Pallas kernels  88 us (96%)
  other arithmetic  1.7 us (2%)
  between operations  1.41 us (2%)
    pallas_call x1, Pallas kernels, body(): pl.pallas_call(kernel, out_shape=jax.ShapeDtypeStruct((32, HEADS * HD), b...  88 us

profile of v1, /device:TPU:56, one launch (start us, length us, event | category | flops | bytes accessed | tf_op | source)
XLA Modules:
  0.0 91.1 jit_solution(3950049925528729940)
XLA Ops:
  0.0 0.0 copy-start
  1.4 0.0 copy-done
  1.4 88.0 %shard_map.64 = bf16[32,4096]{1,0:T(8,128)(2,1)} custom-call(bf16[32,4096]{1,0:T(8,128)(2,1)} %bitcast.10, bf16[32,4096]{1,0:T(8,128)(2,1)} %bitcast.11, bf16[32,4096]{1,0:T(8,128)(2,1)} %bitcast.12, s32[1]{0:T(128)S(6)} %copy.7.cf_ref), custom_call_target="tpu_custom_call" | custom-call | tf_op jit(solution)/shard_map/pallas_call | solution.py:267
  89.4 1.7 %fusion = bf16[1,32,4096]{2,1,0:T(8,128)(2,1)} fusion(bf16[32,4096]{1,0:T(8,128)(2,1)} %shard_map.64, f32[4096]{0:T(1024)S(1)} %bitcast.13), kind=kLoop, calls=%fused_computation.1 | loop fusion | flops 393216 | bytes 540672 | tf_op jit(solution)/shard_map/broadcast_in_dim | solution.py:295
  (1 shorter events, 0.0 us)
Async XLA Ops:
  0.0 1.4 %copy-start = (f32[50,4096]{1,0:T(8,128)S(1)}, f32[50,4096]{1,0:T(8,128)}, u32[]{:S(2)}) copy-start(f32[50,4096]{1,0:T(8,128)} %param.11) | copy-start | bytes 2457604

commit v2 on v1

v2 whole, which is shorter than its diff:
```python
import functools
import math

import jax
import jax.numpy as jnp
from jax import lax
from jax.experimental import pallas as pl
from jax.experimental.pallas import tpu as pltpu
from jax.sharding import Mesh
from jax.sharding import PartitionSpec as P

HEADS = 32
HD = 128
AXES = ("stretch", "z", "yh", "xh", "xl", "co")
SEQ = AXES[1:]
MESH = pl.DeviceIdType.MESH
NEG = -1e30
LOG2 = HD**-0.5 * math.log2(math.e)
NT = (((1,), (1,)), ((), ()))


def to_row(column):
    return jnp.broadcast_to(column, (128, 128)).T[0:1, :]


def to_column(row):
    return jnp.broadcast_to(row, (128, 128)).T[:, 0:1]


def kernel(
    q_in, k_in, v_in, cf_ref, att,
    qb, qp, kb, vb, cfb, cf_in, bias, held, held_max, op, op_in, st, st_in, ob,
    meet, asend, arecv, alocal, gs, gr, hs, hr, os_, or_, rs, rr, rl,
):
    c, z, yh, xh, xl, co = (lax.axis_index(a) for a in AXES)
    g = yh * 2 + xh
    half = z // 4
    head = z * 4 + g

    def dev(c=c, z=z, g=g, xl=xl, co=co):
        return (c, z, g // 2, lax.rem(g, 2), xl, co)

    def gx(d):
        return ((yh + d // 2) % 2) * 2 + (xh + d % 2) % 2

    def zx(d):
        return lax.rem(z + d, 8)

    before = lax.rem(c + 3, 4)
    after = lax.rem(c + 1, 4)
    twin = dev(co=1 - co)
    across = dev(xl=1 - xl)

    def signal(semaphore, partners):
        for partner in partners:
            pl.semaphore_signal(semaphore, inc=1, device_id=partner, device_id_type=MESH)

    barrier = pltpu.get_barrier_semaphore()
    line = [dev(z=zx(d)) for d in (4, 3, 5, 2, 6, 1, 7)]
    others = [dev(g=gx(d)) for d in (3, 2, 1)]
    near = [dev(c=before), dev(c=after), across, twin]
    signal(barrier, line + others + near)
    for slot in range(4):
        vb[slot, :, :, :, HD:] = jnp.ones((8, 4, 32, HD), jnp.bfloat16)
    cfb[...] = jnp.full((8, 128), cf_ref[0], jnp.float32)
    pl.semaphore_wait(barrier, len(line + others + near))
    signal(meet, others)
    pl.semaphore_wait(meet, len(others))

    def remote(src, dst, send, recv, to):
        return pltpu.make_async_remote_copy(
            src_ref=src, dst_ref=dst, send_sem=send, recv_sem=recv, device_id=to, device_id_type=MESH
        )

    def lanes(start, size):
        return pl.ds(pl.multiple_of(start, 128), size)

    sent = []
    far = [(d, e) for d in (4, 3, 5, 2, 6, 1, 7, 0) for e in (3, 2, 1, 0) if (d, e) != (0, 0)]

    def exchange(n, src, dst):
        for d, e in far:
            to_z, to_g = zx(d), gx(e)
            remote(
                src.at[:, lanes((to_z * 4 + to_g) * HD, HD)], dst, asend.at[n], arecv.at[n], dev(z=to_z, g=to_g)
            ).start()
        pltpu.make_async_copy(src.at[:, lanes(head * HD, HD)], dst, alocal.at[n]).start()

    def all_bytes(semaphore):
        area = att.at[:, pl.ds(0, len(far) * HD)]
        return pltpu.make_async_copy(area, area, semaphore)

    def arrived(n):
        all_bytes(arecv.at[n]).wait()
        area = att.at[:, pl.ds(0, HD)]
        pltpu.make_async_copy(area, area, alocal.at[n]).wait()

    def gather(n, buf, cols):
        to_twin = remote(buf.at[0, :, :, :, cols], buf.at[1, :, :, :, cols], gs.at[n, 0], gr.at[n, 0], twin)
        to_across = remote(buf.at[0, :, :, :, cols], buf.at[2, :, :, :, cols], gs.at[n, 1], gr.at[n, 1], across)
        relay = remote(buf.at[2, :, :, :, cols], buf.at[3, :, :, :, cols], gs.at[n, 2], gr.at[n, 2], twin)
        to_across.start()
        to_twin.start()
        sent.extend((to_twin, to_across, relay))
        return to_twin, to_across, relay

    cols = pl.ds(0, HD)
    for slot in range(4):
        vb[slot, :, :, :, HD:] = jnp.ones((8, 4, 32, HD), jnp.bfloat16)
    @pl.when(c == 0)
    def _():
        op_in[...] = jnp.zeros_like(op_in)
        st_in[:, 0:4, :] = jnp.full((2, 4, 128), NEG, jnp.float32)
        st_in[:, 4:8, :] = jnp.zeros((2, 4, 128), jnp.float32)

    exchange(0, q_in, qb.at[z, g])
    exchange(1, k_in, kb.at[0, z, g])
    exchange(2, v_in, vb.at[0, z, g, :, cols])

    arrived(0)
    q_hop = remote(qb, qp, hs.at[0], hr.at[0], dev(c=before))
    cf_hop = remote(cfb, cf_in, hs.at[1], hr.at[1], dev(c=before))

    @pl.when(c > 0)
    def _():
        q_hop.start()
        cf_hop.start()

    arrived(1)
    k_twin, k_across, k_relay = gather(0, kb, cols)
    arrived(2)
    v_twin, v_across, v_relay = gather(1, vb, cols)
    k_across.wait_recv()
    k_relay.start()
    k_twin.wait_recv()
    v_twin.wait_recv()

    def attend(queries, slots, masked, state=None):
        largest, numer = state if state else (None, None)
        for slot in slots:
            for part in range(2):
                keys = kb[slot, part * 4 : part * 4 + 4].reshape(512, HD)
                values = vb[slot, part * 4 : part * 4 + 4].reshape(512, 2 * HD)
                scores = lax.dot_general(queries, keys, NT, preferred_element_type=jnp.float32)
                if masked:
                    scores = scores + bias[slot : slot + 1, part * 512 : part * 512 + 512]
                here = jnp.max(scores, axis=1, keepdims=True)
                updated = here if largest is None else jnp.maximum(largest, here)
                weights = jnp.exp2((scores - updated) * LOG2).astype(jnp.bfloat16)
                more = jnp.dot(weights, values, preferred_element_type=jnp.float32)
                numer = more if largest is None else numer * jnp.exp2((largest - updated) * LOG2) + more
                largest = updated
        return largest, numer

    returns = [
        (
            remote(op.at[pl.ds(i * 4, 4)], op_in.at[pl.ds(i * 4, 4)], os_.at[i], or_.at[i], dev(c=after)),
            remote(st.at[i], st_in.at[i], os_.at[2 + i], or_.at[2 + i], dev(c=after)),
        )
        for i in range(2)
    ]

    def past_queries(i):
        return qp[i * 4 : i * 4 + 4].reshape(512, HD)

    def past_begin(i):
        largest, numer = attend(past_queries(i), (0, 1), True)
        held[i] = numer
        held_max[i] = jnp.broadcast_to(largest, (512, 128))

    @pl.when(c < 3)
    def _():
        q_hop.wait_recv()
        cf_hop.wait_recv()
        cache_from = cf_in[0:1, 0:1]
        for slot in range(4):
            chunk = lax.rem(xl + slot // 2, 2) * 2 + lax.rem(co + slot % 2, 2)
            row = lax.broadcasted_iota(jnp.int32, (1, 1024), 1)
            position = (row // 32) * 128 + chunk * 32 + row % 32
            bias[pl.ds(slot, 1), :] = jnp.where(position.astype(jnp.float32) >= cache_from, 0.0, NEG)
        past_begin(0)

    v_across.wait_recv()
    v_relay.start()

    @pl.when(c < 3)
    def _():
        past_begin(1)

    k_relay.wait_recv()
    v_relay.wait_recv()

    @pl.when(c < 3)
    def _():
        for i in range(2):
            largest, numer = attend(past_queries(i), (2, 3), True, (held_max[i][:, 0:1], held[i]))
            total = numer[:, HD : HD + 1]
            op[pl.ds(i * 4, 4)] = (numer[:, :HD] / total).astype(jnp.bfloat16).reshape(4, 4, 32, HD)
            for n in range(4):
                rows = slice(n * 128, n * 128 + 128)
                st[i, n : n + 1, :] = to_row(largest[rows])
                st[i, n + 4 : n + 5, :] = to_row(total[rows])
            for copy in returns[i]:
                copy.start()

    for i in range(2):
        base = (half + 1 - i) % 2
        rows4 = pl.ds(base * 4, 4)
        largest, numer = attend(qb[rows4].reshape(512, HD), (0, 1, 2, 3), False)
        total = numer[:, HD : HD + 1]

        if i == 0:

            @pl.when(c > 0)
            def _():
                for j in range(2):
                    for copy in returns[j]:
                        copy.wait_recv()

        past = op_in[rows4].reshape(512, HD).astype(jnp.float32)
        stats = st_in[base]
        past_largest = jnp.concatenate([to_column(stats[n : n + 1]) for n in range(4)], 0)
        past_total = jnp.concatenate([to_column(stats[n + 4 : n + 5]) for n in range(4)], 0)
        updated = jnp.maximum(largest, past_largest)
        mine = jnp.exp2((largest - updated) * LOG2)
        theirs = past_total * jnp.exp2((past_largest - updated) * LOG2)
        whole = (numer[:, :HD] * mine + past * theirs) / (total * mine + theirs)
        ob[rows4] = whole.astype(jnp.bfloat16).reshape(4, 4, 32, HD)
        for k in range(4):
            to_z = base * 4 + (z + k) % 4
            for e in (3, 2, 1, 0):
                to_g = gx(e)
                if i == 1 and k == 0 and e == 0:
                    continue
                remote(
                    ob.at[to_z, to_g], att.at[:, lanes(head * HD, HD)], rs.at[0], rr.at[0], dev(z=to_z, g=to_g)
                ).start()
    own = pltpu.make_async_copy(ob.at[z, g], att.at[:, lanes(head * HD, HD)], rl.at[0])
    own.start()
    own.wait()
    all_bytes(rr.at[0]).wait()
    all_bytes(rs.at[0]).wait()
    for n in range(3):
        all_bytes(asend.at[n]).wait()
    for copy in sent:
        copy.wait_send()

    @pl.when(c > 0)
    def _():
        q_hop.wait_send()
        cf_hop.wait_send()

    @pl.when(c < 3)
    def _():
        for i in range(2):
            for copy in returns[i]:
                copy.wait_send()


def body(query_rows, key_rows, value_rows, cache_from, time_index, gate_table):
    bf16, f32, dma = jnp.bfloat16, jnp.float32, pltpu.SemaphoreType.DMA
    vmem = pl.BlockSpec(memory_space=pltpu.VMEM)
    hbm = pl.BlockSpec(memory_space=pltpu.HBM)
    attended = pl.pallas_call(
        kernel,
        out_shape=jax.ShapeDtypeStruct((32, HEADS * HD), bf16),
        in_specs=[hbm, hbm, hbm, pl.BlockSpec(memory_space=pltpu.SMEM)],
        out_specs=vmem,
        scratch_shapes=[
            *[pltpu.VMEM((8, 4, 32, HD), bf16)] * 2,
            pltpu.VMEM((4, 8, 4, 32, HD), bf16),
            pltpu.VMEM((4, 8, 4, 32, 2 * HD), bf16),
            *[pltpu.VMEM((8, 128), f32)] * 2,
            pltpu.VMEM((8, 1024), f32),
            pltpu.VMEM((2, 512, 2 * HD), f32),
            pltpu.VMEM((2, 512, 128), f32),
            *[pltpu.VMEM((8, 4, 32, HD), bf16)] * 2,
            *[pltpu.VMEM((2, 8, 128), f32)] * 2,
            pltpu.VMEM((8, 4, 32, HD), bf16),
            pltpu.SemaphoreType.REGULAR,
            *[dma((3,))] * 3,
            *[dma((2, 3))] * 2,
            *[dma((2,))] * 2,
            *[dma((4,))] * 2,
            *[dma((1,))] * 3,
        ],
        compiler_params=pltpu.CompilerParams(
            collective_id=1, has_side_effects=True
        ),
    )(query_rows[0], key_rows[0], value_rows[0], cache_from)
    gate_row = lax.dynamic_slice_in_dim(gate_table, time_index[0], 1, 0)
    return (attended.astype(jnp.float32) * gate_row).astype(jnp.bfloat16)[None]


def solution(mesh):
    finer = Mesh(mesh.devices.reshape(4, 8, 2, 2, 2, 2), AXES)
    rows = P("stretch", SEQ, None)
    return jax.shard_map(
        body,
        mesh=finer,
        in_specs=(rows, rows, rows, P("stretch"), P("stretch"), P()),
        out_specs=rows,
        check_vma=False,
    )
```

time: 91.3 us -> 78 us (0.85)
  the two profiles are of different devices: /device:TPU:56 before, /device:TPU:1 now
where the time goes in v2:
time: 78 us; the launch traced here: 77.8 us
  Pallas kernels  74.7 us (96%)
  other arithmetic  1.7 us (2%)
  between operations  1.41 us (2%)
    pallas_call x1, Pallas kernels, body(): pl.pallas_call(kernel, out_shape=jax.ShapeDtypeStruct((32, HEADS * HD), b...  74.7 us
    broadcast_in_dim x1, other arithmetic, body(): return (attended.astype(jnp.float32) * gate_row).astype(jnp.bfloat16)[None]  1.7 us

profile of v2, /device:TPU:1, one launch (start us, length us, event | category | flops | bytes accessed | tf_op | source)
XLA Modules:
  0.0 77.8 jit_solution(13125201827352231700)
XLA Ops:
  0.0 0.0 copy-start
  1.4 0.0 copy-done
  1.4 74.7 %shard_map.64 = bf16[32,4096]{1,0:T(8,128)(2,1)} custom-call(bf16[32,4096]{1,0:T(8,128)(2,1)} %bitcast.10, bf16[32,4096]{1,0:T(8,128)(2,1)} %bitcast.11, bf16[32,4096]{1,0:T(8,128)(2,1)} %bitcast.12, s32[1]{0:T(128)S(6)} %copy.7.cf_ref), custom_call_target="tpu_custom_call" | custom-call | tf_op jit(solution)/shard_map/pallas_call | solution.py:264
  76.1 1.7 %fusion = bf16[1,32,4096]{2,1,0:T(8,128)(2,1)} fusion(bf16[32,4096]{1,0:T(8,128)(2,1)} %shard_map.64, f32[4096]{0:T(1024)S(1)} %bitcast.13), kind=kLoop, calls=%fused_computation.1 | loop fusion | flops 393216 | bytes 540672 | tf_op jit(solution)/shard_map/broadcast_in_dim | solution.py:292
  (1 shorter events, 0.0 us)
Async XLA Ops:
  0.0 1.4 %copy-start = (f32[50,4096]{1,0:T(8,128)S(1)}, f32[50,4096]{1,0:T(8,128)}, u32[]{:S(2)}) copy-start(f32[50,4096]{1,0:T(8,128)} %param.11) | copy-start | bytes 2457604

commit v3 on v2

v3 whole, which is shorter than its diff:
```python
import functools
import math

import jax
import jax.numpy as jnp
from jax import lax
from jax.experimental import pallas as pl
from jax.experimental.pallas import tpu as pltpu
from jax.sharding import Mesh
from jax.sharding import PartitionSpec as P

HEADS = 32
HD = 128
AXES = ("stretch", "z", "yh", "xh", "xl", "co")
SEQ = AXES[1:]
MESH = pl.DeviceIdType.MESH
NEG = -1e30
LOG2 = HD**-0.5 * math.log2(math.e)
NT = (((1,), (1,)), ((), ()))


def to_row(column):
    return jnp.broadcast_to(column, (128, 128)).T[0:1, :]


def to_column(row):
    return jnp.broadcast_to(row, (128, 128)).T[:, 0:1]


def kernel(
    q_in, k_in, v_in, cf_ref, att,
    qb, qp, kb, vb, cfb, cf_in, bias, held, held_max, op, op_in, st, st_in, ob,
    asend, arecv, alocal, gs, gr, hs, hr, os_, or_, rs, rr, rl,
):
    c, z, yh, xh, xl, co = (lax.axis_index(a) for a in AXES)
    g = yh * 2 + xh
    half = z // 4
    head = z * 4 + g

    def dev(c=c, z=z, g=g, xl=xl, co=co):
        return (c, z, g // 2, lax.rem(g, 2), xl, co)

    def gx(d):
        return ((yh + d // 2) % 2) * 2 + (xh + d % 2) % 2

    def zx(d):
        return lax.rem(z + d, 8)

    before = lax.rem(c + 3, 4)
    after = lax.rem(c + 1, 4)
    twin = dev(co=1 - co)
    across = dev(xl=1 - xl)

    far = sorted(
        ((d, e) for d in range(8) for e in range(4) if (d, e) != (0, 0)),
        key=lambda p: -(min(p[0], 8 - p[0]) + 4 * (p[1] // 2) + 2 * (p[1] % 2)),
    )
    barrier = pltpu.get_barrier_semaphore()
    partners = [dev(z=zx(d), g=gx(e)) for d, e in far]
    partners += [dev(c=before), dev(c=after), across, twin]
    for partner in partners:
        pl.semaphore_signal(barrier, inc=1, device_id=partner, device_id_type=MESH)
    for slot in range(4):
        vb[slot, :, :, :, :, HD:] = jnp.ones((2, 8, 4, 16, HD), jnp.bfloat16)
    cfb[...] = jnp.full((8, 128), cf_ref[0], jnp.float32)
    pl.semaphore_wait(barrier, len(partners))

    def remote(src, dst, send, recv, to):
        return pltpu.make_async_remote_copy(
            src_ref=src, dst_ref=dst, send_sem=send, recv_sem=recv, device_id=to, device_id_type=MESH
        )

    def lanes(start, size):
        return pl.ds(pl.multiple_of(start, 128), size)

    sent = []

    def exchange(n, rows, src, dst):
        for d, e in far:
            to_z, to_g = zx(d), gx(e)
            remote(
                src.at[rows, lanes((to_z * 4 + to_g) * HD, HD)], dst, asend.at[n], arecv.at[n], dev(z=to_z, g=to_g)
            ).start()
        pltpu.make_async_copy(src.at[rows, lanes(head * HD, HD)], dst, alocal.at[n]).start()

    def all_bytes(semaphore, rows=32):
        area = att.at[0:rows, pl.ds(0, len(far) * HD)]
        return pltpu.make_async_copy(area, area, semaphore)

    def arrived(n, rows=16):
        all_bytes(arecv.at[n], rows).wait()
        area = att.at[0:rows, pl.ds(0, HD)]
        pltpu.make_async_copy(area, area, alocal.at[n]).wait()

    def gather(n, part, buf):
        at = [buf.at[slot, part, :, :, :, cols] for slot in range(4)]
        to_twin = remote(at[0], at[1], gs.at[n, 0], gr.at[n, 0], twin)
        to_across = remote(at[0], at[2], gs.at[n, 1], gr.at[n, 1], across)
        relay = remote(at[2], at[3], gs.at[n, 2], gr.at[n, 2], twin)
        to_across.start()
        to_twin.start()
        sent.extend((to_twin, to_across, relay))
        return to_twin, to_across, relay

    cols = pl.ds(0, HD)
    for slot in range(4):
        vb[slot, :, :, :, :, HD:] = jnp.ones((2, 8, 4, 16, HD), jnp.bfloat16)
    @pl.when(c == 0)
    def _():
        op_in[...] = jnp.zeros_like(op_in)
        st_in[:, 0:4, :] = jnp.full((2, 4, 128), NEG, jnp.float32)
        st_in[:, 4:8, :] = jnp.zeros((2, 4, 128), jnp.float32)

    exchange(0, pl.ds(0, 32), q_in, qb.at[z, g])
    for part in range(2):
        rows = pl.ds(part * 16, 16)
        exchange(1 + 2 * part, rows, k_in, kb.at[0, part, z, g])
        exchange(2 + 2 * part, rows, v_in, vb.at[0, part, z, g, :, cols])

    arrived(0, 32)
    q_hop = remote(qb, qp, hs.at[0], hr.at[0], dev(c=before))
    cf_hop = remote(cfb, cf_in, hs.at[1], hr.at[1], dev(c=before))

    @pl.when(c > 0)
    def _():
        cf_hop.start()
        q_hop.start()

    here_0, here_1, there_0, there_1 = (((s, p), (s + 1, p)) for s in (0, 2) for p in (0, 1))

    def attend(queries, groups, masked, state=None):
        largest, numer = state if state else (None, None)
        for slot, part in groups:
            keys = kb[slot, part].reshape(512, HD)
            values = vb[slot, part].reshape(512, 2 * HD)
            scores = lax.dot_general(queries, keys, NT, preferred_element_type=jnp.float32)
            if masked:
                scores = scores + bias[slot : slot + 1, part * 512 : part * 512 + 512]
            top = jnp.max(scores, axis=1, keepdims=True)
            updated = top if largest is None else jnp.maximum(largest, top)
            weights = jnp.exp2((scores - updated) * LOG2).astype(jnp.bfloat16)
            more = jnp.dot(weights, values, preferred_element_type=jnp.float32)
            numer = more if largest is None else numer * jnp.exp2((largest - updated) * LOG2) + more
            largest = updated
        return largest, numer

    def hold(n, result):
        held_max[n] = jnp.broadcast_to(result[0], (512, 128))
        held[n] = result[1]

    def holding(n):
        return held_max[n][:, 0:1], held[n]

    def queries_of(buf, i):
        return buf[pl.ds(((half + 1 - i) % 2) * 4, 4)].reshape(512, HD)

    def past_more(groups):
        @pl.when(c < 3)
        def _():
            for i in range(2):
                hold(i, attend(queries_of(qp, i), groups, True, holding(i)))

    def returns(i):
        rows4 = pl.ds(((half + 1 - i) % 2) * 4, 4)
        return (
            remote(op.at[rows4], op_in.at[rows4], os_.at[i], or_.at[i], dev(c=after)),
            remote(st.at[i], st_in.at[i], os_.at[2 + i], or_.at[2 + i], dev(c=after)),
        )

    arrived(1)
    k0_twin, k0_across, k0_relay = gather(0, 0, kb)
    arrived(2)
    v0_twin, v0_across, v0_relay = gather(1, 0, vb)
    k0_across.wait_recv()
    k0_relay.start()
    k0_twin.wait_recv()
    v0_twin.wait_recv()
    hold(2, attend(queries_of(qb, 0), here_0, False))
    arrived(3)
    k1_twin, k1_across, k1_relay = gather(2, 1, kb)
    v0_across.wait_recv()
    v0_relay.start()

    @pl.when(c < 3)
    def _():
        q_hop.wait_recv()
        cf_hop.wait_recv()
        cache_from = cf_in[0:1, 0:1]
        for slot in range(4):
            chunk = lax.rem(xl + slot // 2, 2) * 2 + lax.rem(co + slot % 2, 2)
            row = lax.broadcasted_iota(jnp.int32, (1, 1024), 1)
            position = ((row % 512) // 16) * 128 + chunk * 32 + (row // 512) * 16 + row % 16
            bias[pl.ds(slot, 1), :] = jnp.where(position.astype(jnp.float32) >= cache_from, 0.0, NEG)
        for i in range(2):
            hold(i, attend(queries_of(qp, i), here_0, True))

    arrived(4)
    v1_twin, v1_across, v1_relay = gather(3, 1, vb)
    k0_relay.wait_recv()
    v0_relay.wait_recv()
    past_more(there_0)
    k1_across.wait_recv()
    k1_relay.start()
    k1_twin.wait_recv()
    v1_twin.wait_recv()
    past_more(here_1)
    v1_across.wait_recv()
    v1_relay.start()
    hold(3, attend(queries_of(qb, 1), here_0, False))
    k1_relay.wait_recv()
    v1_relay.wait_recv()

    @pl.when(c < 3)
    def _():
        for i in range(2):
            largest, numer = attend(queries_of(qp, i), there_1, True, holding(i))
            total = numer[:, HD : HD + 1]
            rows4 = pl.ds(((half + 1 - i) % 2) * 4, 4)
            op[rows4] = (numer[:, :HD] / total).astype(jnp.bfloat16).reshape(4, 4, 32, HD)
            for n in range(4):
                rows = slice(n * 128, n * 128 + 128)
                st[i, n : n + 1, :] = to_row(largest[rows])
                st[i, n + 4 : n + 5, :] = to_row(total[rows])
            for copy in returns(i):
                copy.start()

    for i in range(2):
        base = (half + 1 - i) % 2
        rows4 = pl.ds(base * 4, 4)
        largest, numer = attend(queries_of(qb, i), there_0 + here_1 + there_1, False, holding(2 + i))
        total = numer[:, HD : HD + 1]

        @pl.when(c > 0)
        def _():
            for copy in returns(i):
                copy.wait_recv()

        past = op_in[rows4].reshape(512, HD).astype(jnp.float32)
        past_largest = jnp.concatenate([to_column(st_in[i, n : n + 1, :]) for n in range(4)], 0)
        past_total = jnp.concatenate([to_column(st_in[i, n + 4 : n + 5, :]) for n in range(4)], 0)
        updated = jnp.maximum(largest, past_largest)
        mine = jnp.exp2((largest - updated) * LOG2)
        theirs = past_total * jnp.exp2((past_largest - updated) * LOG2)
        whole = (numer[:, :HD] * mine + past * theirs) / (total * mine + theirs)
        ob[rows4] = whole.astype(jnp.bfloat16).reshape(4, 4, 32, HD)
        for k in range(4):
            to_z = base * 4 + (z + k) % 4
            for e in (3, 2, 1, 0):
                to_g = gx(e)
                if i == 1 and k == 0 and e == 0:
                    continue
                remote(
                    ob.at[to_z, to_g], att.at[:, lanes(head * HD, HD)], rs.at[0], rr.at[0], dev(z=to_z, g=to_g)
                ).start()
    own = pltpu.make_async_copy(ob.at[z, g], att.at[:, lanes(head * HD, HD)], rl.at[0])
    own.start()
    own.wait()
    all_bytes(rr.at[0]).wait()
    all_bytes(rs.at[0]).wait()
    for n in range(5):
        all_bytes(asend.at[n], 16 if n else 32).wait()
    for copy in sent:
        copy.wait_send()

    @pl.when(c > 0)
    def _():
        q_hop.wait_send()
        cf_hop.wait_send()

    @pl.when(c < 3)
    def _():
        for i in range(2):
            for copy in returns(i):
                copy.wait_send()


def body(query_rows, key_rows, value_rows, cache_from, time_index, gate_table):
    bf16, f32, dma = jnp.bfloat16, jnp.float32, pltpu.SemaphoreType.DMA
    vmem = pl.BlockSpec(memory_space=pltpu.VMEM)
    hbm = pl.BlockSpec(memory_space=pltpu.HBM)
    attended = pl.pallas_call(
        kernel,
        out_shape=jax.ShapeDtypeStruct((32, HEADS * HD), bf16),
        in_specs=[hbm, hbm, hbm, pl.BlockSpec(memory_space=pltpu.SMEM)],
        out_specs=vmem,
        scratch_shapes=[
            *[pltpu.VMEM((8, 4, 32, HD), bf16)] * 2,
            pltpu.VMEM((4, 2, 8, 4, 16, HD), bf16),
            pltpu.VMEM((4, 2, 8, 4, 16, 2 * HD), bf16),
            *[pltpu.VMEM((8, 128), f32)] * 2,
            pltpu.VMEM((8, 1024), f32),
            pltpu.VMEM((4, 512, 2 * HD), f32),
            pltpu.VMEM((4, 512, 128), f32),
            *[pltpu.VMEM((8, 4, 32, HD), bf16)] * 2,
            *[pltpu.VMEM((2, 8, 128), f32)] * 2,
            pltpu.VMEM((8, 4, 32, HD), bf16),
            *[dma((5,))] * 3,
            *[dma((4, 3))] * 2,
            *[dma((2,))] * 2,
            *[dma((4,))] * 2,
            *[dma((1,))] * 3,
        ],
        compiler_params=pltpu.CompilerParams(
            collective_id=1, has_side_effects=True
        ),
    )(query_rows[0], key_rows[0], value_rows[0], cache_from)
    gate_row = lax.dynamic_slice_in_dim(gate_table, time_index[0], 1, 0)
    return (attended.astype(jnp.float32) * gate_row).astype(jnp.bfloat16)[None]


def solution(mesh):
    finer = Mesh(mesh.devices.reshape(4, 8, 2, 2, 2, 2), AXES)
    rows = P("stretch", SEQ, None)
    return jax.shard_map(
        body,
        mesh=finer,
        in_specs=(rows, rows, rows, P("stretch"), P("stretch"), P()),
        out_specs=rows,
        check_vma=False,
    )
```

time: 78 us -> 74.5 us (0.955); the launches traced: 77.8 us -> 73.3 us
  Pallas kernels: 74.7 us -> 70.2 us
    pallas_call x1, Pallas kernels: 74.7 us -> 70.2 us  [body(): pl.pallas_call(kernel, out_shape=jax.ShapeDtypeStruct((32, HEADS * HD), b...]
where the time goes in v3:
time: 74.5 us; the launch traced here: 73.3 us
  Pallas kernels  70.2 us (94%)
  other arithmetic  1.7 us (2%)
  between operations  1.41 us (2%)
    pallas_call x1, Pallas kernels, body(): pl.pallas_call(kernel, out_shape=jax.ShapeDtypeStruct((32, HEADS * HD), b...  70.2 us
    broadcast_in_dim x1, other arithmetic, body(): return (attended.astype(jnp.float32) * gate_row).astype(jnp.bfloat16)[None]  1.7 us

profile of v3, /device:TPU:1, one launch (start us, length us, event | category | flops | bytes accessed | tf_op | source)
XLA Modules:
  0.0 73.3 jit_solution(12012730539659003556)
XLA Ops:
  0.0 0.0 copy-start
  1.4 0.0 copy-done
  1.4 70.2 %shard_map.64 = bf16[32,4096]{1,0:T(8,128)(2,1)} custom-call(bf16[32,4096]{1,0:T(8,128)(2,1)} %bitcast.10, bf16[32,4096]{1,0:T(8,128)(2,1)} %bitcast.11, bf16[32,4096]{1,0:T(8,128)(2,1)} %bitcast.12, s32[1]{0:T(128)S(6)} %copy.7.cf_ref), custom_call_target="tpu_custom_call" | custom-call | tf_op jit(solution)/shard_map/pallas_call | solution.py:281
  71.6 1.7 %fusion = bf16[1,32,4096]{2,1,0:T(8,128)(2,1)} fusion(bf16[32,4096]{1,0:T(8,128)(2,1)} %shard_map.64, f32[4096]{0:T(1024)S(1)} %bitcast.13), kind=kLoop, calls=%fused_computation.1 | loop fusion | flops 393216 | bytes 540672 | tf_op jit(solution)/shard_map/broadcast_in_dim | solution.py:308
  (1 shorter events, 0.0 us)
Async XLA Ops:
  0.0 1.4 %copy-start = (f32[50,4096]{1,0:T(8,128)S(1)}, f32[50,4096]{1,0:T(8,128)}, u32[]{:S(2)}) copy-start(f32[50,4096]{1,0:T(8,128)} %param.11) | copy-start | bytes 2457604

commit v4 on v3

--- a/solution.py
+++ b/solution.py
@@ -301,7 +301,7 @@
             *[dma((1,))] * 3,
         ],
         compiler_params=pltpu.CompilerParams(
-            collective_id=1, has_side_effects=True
+            collective_id=1, has_side_effects=True, vmem_limit_bytes=56_160_000
         ),
     )(query_rows[0], key_rows[0], value_rows[0], cache_from)
     gate_row = lax.dynamic_slice_in_dim(gate_table, time_index[0], 1, 0)

time: 74.5 us -> 72.8 us (0.977)
  other arithmetic: 1.7 us -> 0.75 us
    broadcast_in_dim x1, other arithmetic: 1.7 us -> 0.75 us  [body(): return (attended.astype(jnp.float32) * gate_row).astype(jnp.bfloat16)[None]]
where the time goes in v4:
time: 72.8 us; the launch traced here: 71.6 us
  Pallas kernels  69.5 us (95%)
  between operations  1.41 us (2%)
  other arithmetic  0.75 us (1%)
    pallas_call x1, Pallas kernels, body(): pl.pallas_call(kernel, out_shape=jax.ShapeDtypeStruct((32, HEADS * HD), b...  69.5 us

profile of v4, /device:TPU:1, one launch (start us, length us, event | category | flops | bytes accessed | tf_op | source)
XLA Modules:
  0.0 71.6 jit_solution(5039292463498773482)
XLA Ops:
  0.0 0.0 copy-start
  1.4 0.0 copy-done
  1.4 69.5 %shard_map.64 = bf16[32,4096]{1,0:T(8,128)(2,1)S(1)} custom-call(bf16[32,4096]{1,0:T(8,128)(2,1)} %bitcast.10, bf16[32,4096]{1,0:T(8,128)(2,1)} %bitcast.11, bf16[32,4096]{1,0:T(8,128)(2,1)} %bitcast.12, s32[1]{0:T(128)S(6)} %copy.7.cf_ref), custom_call_target="tpu_custom_call" | custom-call | tf_op jit(solution)/shard_map/pallas_call | solution.py:281
  70.9 0.7 %fusion = bf16[1,32,4096]{2,1,0:T(8,128)(2,1)} fusion(bf16[32,4096]{1,0:T(8,128)(2,1)S(1)} %shard_map.64, f32[4096]{0:T(1024)S(1)} %bitcast.13), kind=kLoop, calls=%fused_computation.1 | loop fusion | flops 393216 | bytes 540672 | tf_op jit(solution)/shard_map/broadcast_in_dim | solution.py:308
  (1 shorter events, 0.0 us)
Async XLA Ops:
  0.0 1.4 %copy-start = (f32[50,4096]{1,0:T(8,128)S(1)}, f32[50,4096]{1,0:T(8,128)}, u32[]{:S(2)}) copy-start(f32[50,4096]{1,0:T(8,128)} %param.11) | copy-start | bytes 2457604

commit v5 on v4

--- a/solution.py
+++ b/solution.py
@@ -243,10 +243,9 @@
         theirs = past_total * jnp.exp2((past_largest - updated) * LOG2)
         whole = (numer[:, :HD] * mine + past * theirs) / (total * mine + theirs)
         ob[rows4] = whole.astype(jnp.bfloat16).reshape(4, 4, 32, HD)
-        for k in range(4):
-            to_z = base * 4 + (z + k) % 4
-            for e in (3, 2, 1, 0):
-                to_g = gx(e)
+        for e in (3, 2, 1, 0):
+            for k in (2, 1, 3, 0):
+                to_z, to_g = base * 4 + (z + k) % 4, gx(e)
                 if i == 1 and k == 0 and e == 0:
                     continue
                 remote(

time: 72.8 us -> 73.1 us (level); the launches traced: 71.6 us -> 73 us
  Pallas kernels: 69.5 us -> 70.8 us
    pallas_call x1, Pallas kernels: 69.5 us -> 70.8 us  [body(): pl.pallas_call(kernel, out_shape=jax.ShapeDtypeStruct((32, HEADS * HD), b...]
where the time goes in v5:
time: 73.1 us; the launch traced here: 73 us
  Pallas kernels  70.8 us (97%)
  between operations  1.41 us (2%)
  other arithmetic  0.75 us (1%)
    pallas_call x1, Pallas kernels, body(): pl.pallas_call(kernel, out_shape=jax.ShapeDtypeStruct((32, HEADS * HD), b...  70.8 us

profile of v5, /device:TPU:1, one launch (start us, length us, event | category | flops | bytes accessed | tf_op | source)
XLA Modules:
  0.0 73.0 jit_solution(1726447361515962422)
XLA Ops:
  0.0 0.0 copy-start
  1.4 0.0 copy-done
  1.4 70.8 %shard_map.64 = bf16[32,4096]{1,0:T(8,128)(2,1)S(1)} custom-call(bf16[32,4096]{1,0:T(8,128)(2,1)} %bitcast.10, bf16[32,4096]{1,0:T(8,128)(2,1)} %bitcast.11, bf16[32,4096]{1,0:T(8,128)(2,1)} %bitcast.12, s32[1]{0:T(128)S(6)} %copy.7.cf_ref), custom_call_target="tpu_custom_call" | custom-call | tf_op jit(solution)/shard_map/pallas_call | solution.py:280
  72.2 0.7 %fusion = bf16[1,32,4096]{2,1,0:T(8,128)(2,1)} fusion(bf16[32,4096]{1,0:T(8,128)(2,1)S(1)} %shard_map.64, f32[4096]{0:T(1024)S(1)} %bitcast.13), kind=kLoop, calls=%fused_computation.1 | loop fusion | flops 393216 | bytes 540672 | tf_op jit(solution)/shard_map/broadcast_in_dim | solution.py:307
  (1 shorter events, 0.0 us)
Async XLA Ops:
  0.0 1.4 %copy-start = (f32[50,4096]{1,0:T(8,128)S(1)}, f32[50,4096]{1,0:T(8,128)}, u32[]{:S(2)}) copy-start(f32[50,4096]{1,0:T(8,128)} %param.11) | copy-start | bytes 2457604
